TPU v7x, 32 devices: a whole 2x2x4 slice. The times are simulated.
32 devices in a mesh: row: 4 (over z), col: 8 (over y, x, core).
Axes of the slice: x: 2, y: 2, z: 4, core: 2. Of those that a mesh axis runs over, the one named last changes fastest.
Arguments:
- state_start: bfloat16 [512, 2048], P('row', 'col'), may hold values from -360 to 360
- actions: int32 [512, 2], P('row'), may hold values from 0 to 17
- targets: bfloat16 [2, 512, 2048], P(None, 'row'), may hold values from -504 to 504
- w_in: bfloat16 [2048, 4096], P('row', 'col'), may hold values from -0.125 to 0.125
- w_out: bfloat16 [4096, 2048], P('col', 'row'), may hold values from -0.09375 to 0.09375
- action_embed: bfloat16 [18, 4096], P(None, 'col'), may hold values from -6 to 6
Outputs:
- grad_w_in: float32 [2048, 4096], P('row', 'col')
- grad_w_out: float32 [4096, 2048], P('col', 'row')
All inputs are finite; a program needn't handle non-finite values.
Results may differ from a plain program's by a relative error of at most 0.035.
Values may be sent and summed in bfloat16 or wider, within the bound.
A program may use at most 64 MiB of HBM per device.

v0:
```python
import jax
import jax.numpy as jnp
from jax import lax
from jax.sharding import PartitionSpec as P

EPS = 1e-06
LOSS_SCALE = 128.0


def silu_grad(pre_act):
    gate_val = jax.nn.sigmoid(pre_act)
    return gate_val * (1.0 + pre_act * (1.0 - gate_val))


def cosine_from(state_f, target_f, self_dot, cross_dot, target_dot):
    inv_state = lax.rsqrt(self_dot + EPS)
    inv_target = lax.rsqrt(target_dot + EPS)
    cosine = cross_dot * inv_state * inv_target
    return -LOSS_SCALE * (
        target_f * inv_state * inv_target - cosine * state_f * inv_state * inv_state
    )


def shared_cosine(state, target):
    state_f = state.astype(jnp.float32)
    target_f = target.astype(jnp.float32)
    self_dot, cross_dot, target_dot = lax.psum(
        (
            jnp.sum(state_f * state_f, axis=-1),
            jnp.sum(state_f * target_f, axis=-1),
            jnp.sum(target_f * target_f, axis=-1),
        ),
        "col",
    )
    return cosine_from(
        state_f, target_f, self_dot[:, None], cross_dot[:, None], target_dot[:, None]
    )


def on_device(state_start, actions, targets, w_in, w_out, action_embed):
    unroll_steps = targets.shape[0]
    col_width = state_start.shape[1]
    w_in_panel = lax.all_gather(w_in, "row", axis=0, tiled=True)
    w_out_panel = lax.all_gather(w_out, "row", axis=1, tiled=True)
    col_start = lax.axis_index("col") * col_width
    action_ids = jnp.arange(action_embed.shape[0], dtype=jnp.int32)
    contract_last = (((1,), (1,)), ((), ()))
    current = state_start
    full_states = []
    pre_list = []
    hidden_list = []
    cos_terms = []
    for unroll in range(unroll_steps):
        full_rows = lax.all_gather(current, "col", axis=1, tiled=True)
        onehot = (actions[:, unroll][:, None] == action_ids[None, :]).astype(jnp.bfloat16)
        pre_act = jnp.dot(full_rows, w_in_panel, preferred_element_type=jnp.float32) + jnp.dot(
            onehot, action_embed, preferred_element_type=jnp.float32
        )
        hidden = jax.nn.silu(pre_act).astype(jnp.bfloat16)
        partial_value = jnp.dot(hidden, w_out_panel, preferred_element_type=jnp.float32)
        target = targets[unroll]
        branch = lax.psum_scatter(
            partial_value.astype(jnp.bfloat16), "col", scatter_dimension=1, tiled=True
        ).astype(jnp.float32)
        current = (current.astype(jnp.float32) + branch).astype(jnp.bfloat16)
        target_slice = lax.dynamic_slice_in_dim(target, col_start, col_width, 1)
        cos_terms.append(shared_cosine(current, target_slice))
        full_states.append(full_rows)
        pre_list.append(pre_act)
        hidden_list.append(hidden)
    state_grad = cos_terms[unroll_steps - 1].astype(jnp.bfloat16)
    grad_list = [None] * unroll_steps
    hid_grads = [None] * unroll_steps
    for unroll in reversed(range(unroll_steps)):
        grad_rows = lax.all_gather(state_grad, "col", axis=1, tiled=True)
        back = lax.dot_general(
            grad_rows, w_out_panel, contract_last, preferred_element_type=jnp.float32
        )
        hid_grad = (back * silu_grad(pre_list[unroll])).astype(jnp.bfloat16)
        grad_list[unroll] = grad_rows
        hid_grads[unroll] = hid_grad
        if unroll > 0:
            input_part = lax.dot_general(
                hid_grad, w_in_panel, contract_last, preferred_element_type=jnp.float32
            )
            summed = lax.psum_scatter(
                input_part.astype(jnp.bfloat16), "col", scatter_dimension=1, tiled=True
            ).astype(jnp.float32)
            state_grad = (state_grad.astype(jnp.float32) + summed + cos_terms[unroll - 1]).astype(
                jnp.bfloat16
            )
    grad_stack = jnp.stack(grad_list)
    hidden_stack = jnp.stack(hidden_list)
    state_stack = jnp.stack(full_states)
    hid_stack = jnp.stack(hid_grads)
    grad_feature_blocks = lax.all_to_all(grad_stack, "row", split_axis=2, concat_axis=1, tiled=True)
    hidden_all = lax.all_gather(hidden_stack, "row", axis=1, tiled=True)
    grad_w_out = jnp.einsum(
        "kbf,kbd->fd", hidden_all, grad_feature_blocks, preferred_element_type=jnp.float32
    )
    state_feature_blocks = lax.all_to_all(
        state_stack, "row", split_axis=2, concat_axis=1, tiled=True
    )
    hid_all = lax.all_gather(hid_stack, "row", axis=1, tiled=True)
    grad_w_in = jnp.einsum(
        "kbd,kbf->df", state_feature_blocks, hid_all, preferred_element_type=jnp.float32
    )
    return (grad_w_in, grad_w_out)


def solution(mesh):
    in_specs = (
        P("row", "col"),
        P("row", None),
        P(None, "row", None),
        P("row", "col"),
        P("col", "row"),
        P(None, "col"),
    )
    out_specs = (P("row", "col"), P("col", "row"))
    return jax.shard_map(
        on_device, mesh=mesh, in_specs=in_specs, out_specs=out_specs, check_vma=False
    )
```

profile of v0, /device:TPU:0, one launch (start us, length us, event | category | flops | bytes accessed | tf_op | source)
XLA Modules:
  0.0 336.0 jit_solution(11510671725148091114)
XLA Ops:
  8.7 12.7 %all_gather.24 = bf16[128,2048]{1,0:T(8,128)(2,1)S(1)} all-gather(bf16[128,256]{1,0:T(8,128)(2,1)} %param.6), channel_id=1, replica_groups=mesh['row'=4,'col'=8] {'col'}, dimensions={1}, use_global_device_ids=true | all-gather | bytes 589824 | tf_op jit(solution)/shard_map/all_gather | solution.py:54
  22.4 35.6 %all-gather.5.cloned.1.call-done = bf16[2048,512]{1,0:T(8,128)(2,1)} async-done(((bf16[512,512]{1,0:T(8,128)(2,1)}), bf16[2048,512]{1,0:T(8,128)(2,1)}) %all-gather.5.cloned.1.call-update) | async-done | bytes 2097168 | tf_op jit(solution)/shard_map/all_gather | solution.py:43
  58.0 2.0 convolution_add_fusion.1
  60.0 44.0 %all-gather.7.cloned.1.call-done = bf16[512,2048]{1,0:T(8,128)(2,1)} async-done(((bf16[512,512]{1,0:T(8,128)(2,1)}), bf16[512,2048]{1,0:T(8,128)(2,1)}) %all-gather.7.cloned.1.call-update) | async-done | bytes 2097168 | tf_op jit(solution)/shard_map/all_gather | solution.py:44
  104.0 2.9 convolution_convert_fusion.2
  107.9 2.1 fusion.29
  110.0 30.6 %reduce-scatter.4.cloned.1.call-done = bf16[128,256]{1,0:T(8,128)(2,1)} async-done(((bf16[128,2048]{1,0:T(8,128)(2,1)}), bf16[128,256]{1,0:T(8,128)(2,1)}) %reduce-scatter.4.cloned.1.call-update) | async-done | bytes 65552 | tf_op jit(solution)/shard_map/reduce_scatter | solution.py:62
  141.8 10.9 %all_gather.27 = bf16[128,2048]{1,0:T(8,128)(2,1)S(1)} all-gather(bf16[128,256]{1,0:T(8,128)(2,1)S(1)} %get-tuple-element.14), channel_id=1, replica_groups=mesh['row'=4,'col'=8] {'col'}, dimensions={1}, use_global_device_ids=true | all-gather | bytes 589824 | tf_op jit(solution)/shard_map/all_gather | solution.py:54
  152.7 2.1 convolution_add_fusion
  154.8 2.2 convolution_convert_fusion.1
  157.1 34.2 %reduce-scatter.6.cloned.1.call-done = bf16[128,256]{1,0:T(8,128)(2,1)} async-done(((bf16[128,2048]{1,0:T(8,128)(2,1)}), bf16[128,256]{1,0:T(8,128)(2,1)}) %reduce-scatter.6.cloned.1.call-update) | async-done | bytes 65552 | tf_op jit(solution)/shard_map/reduce_scatter | solution.py:62
  192.3 12.1 %all-reduce = (f32[128]{0:T(128)S(1)}, f32[128]{0:T(128)S(1)}, f32[128]{0:T(128)S(1)}, f32[128]{0:T(128)S(1)}, f32[128]{0:T(128)S(1)}, /*index=5*/f32[128]{0:T(128)S(1)}) all-reduce(f32[128]{0:T(128)S(1)} %get-tuple-element.5, f32[128]{0:T(128)S(1)} %get-tuple-element.6, ...), channel_id=1, replica_groups=mesh['row'=4,'col'=8] {'col'}, use_global_device_ids=true, to_apply=%region_7.8 | all-reduce | flops 768 | bytes 6144 | tf_op jit(solution)/shard_map/psum | solution.py:27
  206.1 10.9 %all_gather.28 = bf16[128,2048]{1,0:T(8,128)(2,1)S(1)} all-gather(bf16[128,256]{1,0:T(8,128)(2,1)S(1)} %fusion.8), channel_id=1, replica_groups=mesh['row'=4,'col'=8] {'col'}, dimensions={1}, use_global_device_ids=true | all-gather | bytes 589824 | tf_op jit(solution)/shard_map/all_gather | solution.py:75
  217.8 2.4 fusion
  222.6 2.0 copy.11
  224.6 4.9 %all-to-all-start = ((bf16[2,128,2048]{1,0,2:T(2,128)(2,1)}), bf16[2,128,2048]{1,0,2:T(2,128)(2,1)S(1)}, u32[]{:S(2)}, u32[]{:S(2)}) async-start(bf16[2,128,2048]{1,0,2:T(2,128)(2,1)} %copy.11), calls=%async_computation.1 | async-start | bytes 2097152 | tf_op jit(solution)/shard_map/all_to_all | solution.py:101
  231.4 25.5 %reduce-scatter.8.cloned.1.call-done = bf16[128,256]{1,0:T(8,128)(2,1)} async-done(((bf16[128,2048]{1,0:T(8,128)(2,1)}), bf16[128,256]{1,0:T(8,128)(2,1)}) %reduce-scatter.8.cloned.1.call-update) | async-done | bytes 65552 | tf_op jit(solution)/shard_map/reduce_scatter | solution.py:86
  258.0 10.9 %all_gather.29 = bf16[128,2048]{1,0:T(8,128)(2,1)S(1)} all-gather(bf16[128,256]{1,0:T(8,128)(2,1)S(1)} %fusion.16), channel_id=1, replica_groups=mesh['row'=4,'col'=8] {'col'}, dimensions={1}, use_global_device_ids=true | all-gather | bytes 589824 | tf_op jit(solution)/shard_map/all_gather | solution.py:75
  271.0 4.6 %all-to-all-start.1 = ((bf16[2,128,2048]{1,0,2:T(2,128)(2,1)}), bf16[2,128,2048]{1,0,2:T(2,128)(2,1)S(1)}, u32[]{:S(2)}, u32[]{:S(2)}) async-start(bf16[2,128,2048]{1,0,2:T(2,128)(2,1)} %copy.13), calls=%async_computation.4 | async-start | bytes 2097152 | tf_op jit(solution)/shard_map/all_to_all | solution.py:96
  275.6 2.5 fusion.2
  280.1 33.4 %all-to-all-done.1 = bf16[2,128,2048]{1,0,2:T(2,128)(2,1)S(1)} async-done(((bf16[2,128,2048]{1,0,2:T(2,128)(2,1)}), bf16[2,128,2048]{1,0,2:T(2,128)(2,1)S(1)}, u32[]{:S(2)}, u32[]{:S(2)}) %all-to-all-start.1) | async-done | bytes 1048608 | tf_op jit(solution)/shard_map/all_to_all | solution.py:96
  314.3 2.9 convolution_bitcast_fusion
  317.2 9.0 %all-gather.9.cloned.1.call-done = bf16[2,512,512]{2,1,0:T(8,128)(2,1)} async-done(((bf16[2,128,512]{2,1,0:T(8,128)(2,1)}), bf16[2,512,512]{2,1,0:T(8,128)(2,1)}) %all-gather.9.cloned.1.call-update) | async-done | bytes 1048592 | tf_op jit(solution)/shard_map/all_gather | solution.py:104
  326.2 2.9 convolution_bitcast_fusion.1
  (56 shorter events, 18.3 us)
Async XLA Ops:
  7.2 15.0 %copy-start = (bf16[18,512]{1,0:T(8,128)(2,1)S(1)}, bf16[18,512]{1,0:T(8,128)(2,1)}, u32[]{:S(2)}) copy-start(bf16[18,512]{1,0:T(8,128)(2,1)} %param.11) | copy-start | bytes 55300
  7.2 50.8 %all-gather.5.cloned.1.call-start = ((), (), s32[]{:S(2)}) async-start(), calls=%async_computation.5 | async-start | bytes 2621440 | tf_op jit(solution)/shard_map/all_gather | solution.py:43
  7.9 96.1 %all-gather.7.cloned.1.call-start = ((), (), s32[]{:S(2)}) async-start(), calls=%async_computation.6 | async-start | bytes 2621440 | tf_op jit(solution)/shard_map/all_gather | solution.py:44
  8.7 132.0 %reduce-scatter.4.cloned.1.call-start = ((), (), s32[]{:S(2)}) async-start(), calls=%async_computation.7 | async-start | bytes 589824 | tf_op jit(solution)/shard_map/reduce_scatter | solution.py:62
  106.9 45.8 %copy-start.1 = (bf16[2048,512]{1,0:T(8,128)(2,1)S(1)}, bf16[2048,512]{1,0:T(8,128)(2,1)}, u32[]{:S(2)}) copy-start(bf16[2048,512]{1,0:T(8,128)(2,1)} %all-gather.5.cloned.1.call-done) | copy-start | bytes 6291460
  106.9 84.4 %reduce-scatter.6.cloned.1.call-start = ((), (), s32[]{:S(2)}) async-start(), calls=%async_computation.8 | async-start | bytes 589824 | tf_op jit(solution)/shard_map/reduce_scatter | solution.py:62
  110.0 31.7 %copy-start.4 = (bf16[1,128,2048]{2,1,0:T(8,128)(2,1)}, bf16[1,128,2048]{2,1,0:T(8,128)(2,1)S(1)}, u32[]{:S(2)}) copy-start(bf16[1,128,2048]{2,1,0:T(8,128)(2,1)S(1)} %get-tuple-element.16) | copy-start | bytes 1572868
  140.6 14.2 %copy-start.9 = (bf16[512,2048]{1,0:T(8,128)(2,1)S(1)}, bf16[512,2048]{1,0:T(8,128)(2,1)}, u32[]{:S(2)}) copy-start(bf16[512,2048]{1,0:T(8,128)(2,1)} %all-gather.7.cloned.1.call-done) | copy-start | bytes 6291460
  157.0 99.9 %reduce-scatter.8.cloned.1.call-start = ((), (), s32[]{:S(2)}) async-start(), calls=%async_computation.9 | async-start | bytes 589824 | tf_op jit(solution)/shard_map/reduce_scatter | solution.py:86
  205.5 0.6 copy-start.5
  217.0 0.8 copy-start.2
  220.2 0.6 copy-start.7
  224.6 32.3 %copy-start.6 = (bf16[128,256]{1,0:T(8,128)(2,1)S(1)}, bf16[128,256]{1,0:T(8,128)(2,1)}, u32[]{:S(2)}) copy-start(bf16[128,256]{1,0:T(8,128)(2,1)} %copy-done.5) | copy-start | bytes 196612
  224.6 44.2 %copy-start.3 = (bf16[128,2048]{1,0:T(8,128)(2,1)S(1)}, bf16[128,2048]{1,0:T(8,128)(2,1)}, u32[]{:S(2)}) copy-start(bf16[128,2048]{1,0:T(8,128)(2,1)} %copy-done.2) | copy-start | bytes 1572868
  224.6 46.3 %all-to-all-start = ((bf16[2,128,2048]{1,0,2:T(2,128)(2,1)}), bf16[2,128,2048]{1,0,2:T(2,128)(2,1)S(1)}, u32[]{:S(2)}, u32[]{:S(2)}) async-start(bf16[2,128,2048]{1,0,2:T(2,128)(2,1)} %copy.11), calls=%async_computation.1 | async-start | bytes 2097152 | tf_op jit(solution)/shard_map/all_to_all | solution.py:101
  229.5 84.8 %all-gather.11.cloned.1.call-start = ((), (), s32[]{:S(2)}) async-start(), calls=%async_computation.11 | async-start | bytes 1310720 | tf_op jit(solution)/shard_map/all_gather | solution.py:97
  271.0 42.5 %all-to-all-start.1 = ((bf16[2,128,2048]{1,0,2:T(2,128)(2,1)}), bf16[2,128,2048]{1,0,2:T(2,128)(2,1)S(1)}, u32[]{:S(2)}, u32[]{:S(2)}) async-start(bf16[2,128,2048]{1,0,2:T(2,128)(2,1)} %copy.13), calls=%async_computation.4 | async-start | bytes 2097152 | tf_op jit(solution)/shard_map/all_to_all | solution.py:96
  275.6 2.5 copy-start.8
  275.6 50.7 %all-gather.9.cloned.1.call-start = ((), (), s32[]{:S(2)}) async-start(), calls=%async_computation.10 | async-start | bytes 1310720 | tf_op jit(solution)/shard_map/all_gather | solution.py:104
Sparse Core Ops, SparseCore 0:
  9.6 48.3 all-gather.4
  59.5 44.4 all-gather.6
  107.7 32.8 reduce-scatter.3
  157.1 34.0 reduce-scatter.5
  222.6 34.2 reduce-scatter.7
  258.4 37.5 all-gather.10
  297.5 28.6 all-gather.8
where the time goes:
time: 337 us; the launch traced here: 336 us
  waiting for transfers between devices  214 us (64%)
  blocking collectives  57.5 us (17%)
  matrix products  22.8 us (7%)
  between operations  14.3 us (4%)
  local copies, waits for them, and re-layouts  11 us (3%)
  starting transfers between devices  9.7 us (3%)
  other arithmetic  6.97 us (2%)
    reduce_scatter x2, waiting for transfers between devices, on_device(): lax.psum_scatter(partial_value.astype(jnp.bfloat16), 'col', scatter_dimen...  64.8 us
    all_gather x1, waiting for transfers between devices, on_device(): w_out_panel = lax.all_gather(w_out, 'row', axis=1, tiled=True)  44 us
    all_gather x1, waiting for transfers between devices, on_device(): w_in_panel = lax.all_gather(w_in, 'row', axis=0, tiled=True)  35.6 us
    all_to_all x1, waiting for transfers between devices, on_device(): lax.all_to_all(grad_stack, 'row', split_axis=2, concat_axis=1, tiled=True)  33.4 us
    reduce_scatter x1, waiting for transfers between devices, on_device(): lax.psum_scatter(input_part.astype(jnp.bfloat16), 'col', scatter_dimensio...  25.5 us
    all_gather x2, blocking collectives, on_device(): full_rows = lax.all_gather(current, 'col', axis=1, tiled=True)  23.6 us
    all_gather x2, blocking collectives, on_device(): grad_rows = lax.all_gather(state_grad, 'col', axis=1, tiled=True)  21.8 us
    psum x1, blocking collectives, shared_cosine(): lax.psum((jnp.sum(state_f * state_f, axis=-1), jnp.sum(state_f * target_f...  12.1 us
  transfers between devices with their start and end apart: 9, of which 7 were waited for; matrix products, arithmetic and copies ran while one was open for 6% of the time, Pallas kernels for 0%

commit v1 on v0

--- a/solution.py
+++ b/solution.py
@@ -1,10 +1,17 @@
+import functools
+
 import jax
 import jax.numpy as jnp
 from jax import lax
+from jax.experimental import pallas as pl
+from jax.experimental.pallas import tpu as pltpu
 from jax.sharding import PartitionSpec as P
 
 EPS = 1e-06
 LOSS_SCALE = 128.0
+MESH = pl.DeviceIdType.MESH
+F32 = jnp.float32
+BF16 = jnp.bfloat16
 
 
 def silu_grad(pre_act):
@@ -37,7 +44,7 @@
     )
 
 
-def on_device(state_start, actions, targets, w_in, w_out, action_embed):
+def gathered(state_start, actions, targets, w_in, w_out, action_embed):
     unroll_steps = targets.shape[0]
     col_width = state_start.shape[1]
     w_in_panel = lax.all_gather(w_in, "row", axis=0, tiled=True)
@@ -108,7 +115,318 @@
     return (grad_w_in, grad_w_out)
 
 
+def sem_plan(nr, nc):
+    at = {}
+    total = 0
+    for name, count in (
+        [("start", 2 * nr), ("targets", nr)]
+        + [(f"cag{i}", nr * nc) for i in range(4)]
+        + [(f"zrs{i}", nr) for i in range(4)]
+        + [(f"zag{i}", nr) for i in range(4)]
+        + [(f"crs{i}", nr * nc) for i in range(3)]
+        + [(f"dot{i}", nr) for i in range(2)]
+    ):
+        at[name] = total
+        total += count
+    return at, total
+
+
+def sends_in_all(nr, nc):
+    return nc + (nr - 1) * (1 + 4 + 4 + 2) + (4 + 3) * nr * (nc - 1)
+
+
+def kernel(
+    nr, nc, st, act, tg, wi, wo, emb, gwi, gwo,
+    s0p, tgp, sfull, hfull, efull, gfull, psend, zr, ysend, cr, own, pre, dsend, dz,
+    send_sem, recv_sem,
+):
+    r, c = lax.axis_index("row"), lax.axis_index("col")
+    piece, df = sfull.shape[3], sfull.shape[4]
+    rb = nc * piece
+    at, _ = sem_plan(nr, nc)
+    started = []
+    unused = iter(range(10000))
+
+    def zpeer(o):
+        return lax.rem(r + o, nr)
+
+    def cpeer(o):
+        return lax.rem(c + o, nc)
+
+    def copy(src, dst, sem, slot, dev):
+        return pltpu.make_async_remote_copy(
+            src_ref=src, dst_ref=dst, send_sem=send_sem.at[sem], recv_sem=recv_sem.at[slot],
+            device_id=dev, device_id_type=MESH,
+        )
+
+    def send(src, dst, slot, dev):
+        out = copy(src, dst, next(unused), slot, dev)
+        out.start()
+        started.append(out)
+
+    def arrived(dst, slot, dev):
+        copy(dst, dst, 0, slot, dev).wait_recv()
+
+    barrier = pltpu.get_barrier_semaphore()
+    for o in range(1, nr):
+        pl.semaphore_signal(barrier, inc=1, device_id=(zpeer(o), c), device_id_type=MESH)
+    for o in range(1, nc):
+        pl.semaphore_signal(barrier, inc=1, device_id=(r, cpeer(o)), device_id_type=MESH)
+    home = lax.div(c, 2)
+    half = lax.rem(c, 2)
+    for hf in range(2):
+        for o in range(1, nr):
+            pl.semaphore_signal(
+                barrier, inc=1, device_id=(zpeer(o), 2 * r + hf), device_id_type=MESH
+            )
+
+        @pl.when(2 * r + hf != c)
+        def _():
+            pl.semaphore_signal(barrier, inc=1, device_id=(r, 2 * r + hf), device_id_type=MESH)
+
+    away = jnp.where(home != r, 1, 0)
+    pl.semaphore_wait(barrier, (nr - 1) + (nc - 1) + (nc - 1) + away)
+
+    for o in range(1, nc):
+        j = cpeer(o)
+        send(st.at[j], s0p.at[half, r], at["start"] + half * nr + r, (home, j))
+    keep = next(unused)
+
+    @pl.when(home != r)
+    def _():
+        copy(st.at[c], s0p.at[half, r], keep, at["start"] + half * nr + r, (home, c)).start()
+
+    @pl.when(home == r)
+    def _():
+        s0p[half, r] = st[c]
+
+    for hf in range(2):
+        for o in range(1, nr):
+            b = zpeer(o)
+            arrived(s0p.at[hf, b], at["start"] + hf * nr + b, (b, 2 * r + hf))
+
+        @pl.when(2 * r + hf != c)
+        def _():
+            arrived(s0p.at[hf, r], at["start"] + hf * nr + r, (r, 2 * r + hf))
+
+    order = [zpeer(o) for o in range(1, nr)] + [r]
+    back_order = [r] + [zpeer(o) for o in range(1, nr)]
+
+    def spread(full, name, b):
+        for o in range(1, nc):
+            send(full.at[b, c], full.at[b, c], at[name] + c * nr + b, (r, cpeer(o)))
+
+    def collect(full, name, b):
+        for o in range(1, nc):
+            j = cpeer(o)
+            arrived(full.at[b, j], at[name] + j * nr + b, (r, j))
+
+    for b in order:
+        sfull[0, b, c] = jnp.concatenate([s0p[0, b], s0p[1, b]], axis=-1)
+        spread(sfull.at[0], "cag0", b)
+
+    for o in range(1, nr):
+        b = zpeer(o)
+        send(
+            tg.at[:, c, :, pl.ds(pl.multiple_of(b * df, df), df)],
+            tgp.at[r], at["targets"] + r, (b, c),
+        )
+    tgp[r] = tg[:, c, :, pl.ds(pl.multiple_of(r * df, df), df)]
+
+    def mm(a, b, dims=((1,), (0,))):
+        return lax.dot_general(a, b, (dims, ((), ())), preferred_element_type=F32)
+
+    def reduce_rows(full, name, weight, dims, phase):
+        for o in range(1, nr):
+            b = zpeer(o)
+            collect(full, name, b)
+            term = mm(full[b].reshape(rb, df), weight[...], dims)
+            psend[phase, b] = term.astype(BF16)
+            send(psend.at[phase, b], zr.at[phase, r], at[f"zrs{phase}"] + r, (b, c))
+        collect(full, name, r)
+        return mm(full[r].reshape(rb, df), weight[...], dims)
+
+    def reduced(total, phase):
+        for o in range(1, nr):
+            b = zpeer(o)
+            arrived(zr.at[phase, b], at[f"zrs{phase}"] + b, (b, c))
+            total = total + zr[phase, b].astype(F32)
+        return total
+
+    def share_rows(full, phase):
+        for o in range(1, nr):
+            send(full.at[r], full.at[r], at[f"zag{phase}"] + r, (zpeer(o), c))
+
+    def shared(full, phase, b):
+        arrived(full.at[b], at[f"zag{phase}"] + b, (b, c))
+
+    def group_terms(full, zphase, weight, dims, phase):
+        for i, b in enumerate(back_order):
+            if i:
+                shared(full, zphase, b)
+            term = mm(full[b], weight[...], dims).astype(BF16)
+            ysend[phase, b] = term.reshape(nc, piece, df)
+            for o in range(1, nc):
+                j = cpeer(o)
+                send(ysend.at[phase, b, j], cr.at[phase, b, c], at[f"crs{phase}"] + c * nr + b, (r, j))
+
+    def group_total(phase, b):
+        total = ysend[phase, b, c].astype(F32)
+        for o in range(1, nc):
+            j = cpeer(o)
+            arrived(cr.at[phase, b, j], at[f"crs{phase}"] + j * nr + b, (r, j))
+            total = total + cr[phase, b, j].astype(F32)
+        return total
+
+    lane = lax.broadcasted_iota(jnp.int32, (piece, 128), 1)
+
+    def dots(u):
+        for b in back_order:
+            s = own[u, b].astype(F32)
+            t = tgp[b, u].astype(F32)
+            ss = jnp.sum(s * s, axis=-1, keepdims=True)
+            sc = jnp.sum(s * t, axis=-1, keepdims=True)
+            tt = jnp.sum(t * t, axis=-1, keepdims=True)
+            both = jnp.where(lane == 0, ss, jnp.where(lane == 1, sc, tt))
+            dsend[u, b] = both
+        dz[u, r] = dsend[u]
+        for o in range(1, nr):
+            send(dsend.at[u], dz.at[u, r], at[f"dot{u}"] + r, (zpeer(o), c))
+
+    def dots_in(u):
+        for o in range(1, nr):
+            b = zpeer(o)
+            arrived(dz.at[u, b], at[f"dot{u}"] + b, (b, c))
+
+    def cosine(u, b):
+        total = dz[u, 0, b]
+        for i in range(1, nr):
+            total = total + dz[u, i, b]
+        return cosine_from(
+            own[u, b].astype(F32), tgp[b, u].astype(F32),
+            total[:, 0:1], total[:, 1:2], total[:, 2:3],
+        )
+
+    ids = lax.broadcasted_iota(jnp.int32, (rb, emb.shape[0]), 1)
+    plain, flipped, over_rows = ((1,), (0,)), ((1,), (1,)), ((0,), (0,))
+
+    for u in range(2):
+        total = reduce_rows(sfull.at[u], f"cag{u}", wi, plain, u)
+        onehot = (act[:, u:u + 1] == ids).astype(F32).astype(BF16)
+        total = total + mm(onehot, emb[...])
+        if u == 1:
+            dots(0)
+        total = reduced(total, u)
+        pre[u] = total
+        hfull[u, r] = (total * jax.nn.sigmoid(total)).astype(BF16)
+        share_rows(hfull.at[u], u)
+        if u == 0:
+            for o in range(1, nr):
+                b = zpeer(o)
+                arrived(tgp.at[b], at["targets"] + b, (b, c))
+        group_terms(hfull.at[u], u, wo, plain, u)
+        for b in back_order:
+            new = (sfull[u, b, c].astype(F32) + group_total(u, b)).astype(BF16)
+            own[u, b] = new
+            if u == 0:
+                sfull[1, b, c] = new
+                spread(sfull.at[1], "cag1", b)
+
+    dots(1)
+    dots_in(1)
+    for b in order:
+        gfull[1, b, c] = cosine(1, b).astype(BF16)
+        spread(gfull.at[1], "cag2", b)
+    for u in (1, 0):
+        total = reduce_rows(gfull.at[u], f"cag{3 - u}", wo, flipped, 3 - u)
+        total = reduced(total, 3 - u)
+        efull[u, r] = (total * silu_grad(pre[u])).astype(BF16)
+        share_rows(efull.at[u], 3 - u)
+        if u == 1:
+            group_terms(efull.at[1], 2, wi, flipped, 2)
+            dots_in(0)
+            for b in back_order:
+                summed = gfull[1, b, c].astype(F32) + group_total(2, b) + cosine(0, b)
+                gfull[0, b, c] = summed.astype(BF16)
+                spread(gfull.at[0], "cag3", b)
+            gwo[...] = mm(hfull[1].reshape(nr * rb, -1), gfull[1].reshape(nr * rb, df), over_rows)
+            gwi[...] = mm(sfull[1].reshape(nr * rb, df), efull[1].reshape(nr * rb, -1), over_rows)
+    gwo[...] += mm(hfull[0].reshape(nr * rb, -1), gfull[0].reshape(nr * rb, df), over_rows)
+    for b in order[:-1]:
+        shared(efull.at[0], 3, b)
+    gwi[...] += mm(sfull[0].reshape(nr * rb, df), efull[0].reshape(nr * rb, -1), over_rows)
+
+    for out in started:
+        out.wait_send()
+
+    @pl.when(home != r)
+    def _():
+        copy(st.at[c], s0p.at[half, r], keep, at["start"] + half * nr + r, (home, c)).wait_send()
+
+
+def stationary(nr, nc, state_start, actions, targets, w_in, w_out, action_embed):
+    rb, sw = state_start.shape
+    piece = rb // nc
+    df, fc = w_in.shape
+    vm = pl.BlockSpec(memory_space=pltpu.VMEM)
+    _, receives = sem_plan(nr, nc)
+    return pl.pallas_call(
+        functools.partial(kernel, nr, nc),
+        out_shape=(
+            jax.ShapeDtypeStruct((df, fc), F32),
+            jax.ShapeDtypeStruct((fc, df), F32),
+        ),
+        in_specs=[vm] * 6,
+        out_specs=(vm, vm),
+        scratch_shapes=[
+            pltpu.VMEM((2, nr, piece, sw), BF16),
+            pltpu.VMEM((nr, 2, piece, df), BF16),
+            pltpu.VMEM((2, nr, nc, piece, df), BF16),
+            pltpu.VMEM((2, nr, rb, fc), BF16),
+            pltpu.VMEM((2, nr, rb, fc), BF16),
+            pltpu.VMEM((2, nr, nc, piece, df), BF16),
+            pltpu.VMEM((4, nr, rb, fc), BF16),
+            pltpu.VMEM((4, nr, rb, fc), BF16),
+            pltpu.VMEM((3, nr, nc, piece, df), BF16),
+            pltpu.VMEM((3, nr, nc, piece, df), BF16),
+            pltpu.VMEM((2, nr, piece, df), BF16),
+            pltpu.VMEM((2, rb, fc), F32),
+            pltpu.VMEM((2, nr, piece, 128), F32),
+            pltpu.VMEM((2, nr, nr, piece, 128), F32),
+            pltpu.SemaphoreType.DMA((sends_in_all(nr, nc),)),
+            pltpu.SemaphoreType.DMA((receives,)),
+        ],
+        compiler_params=pltpu.CompilerParams(
+            collective_id=0, has_side_effects=True, vmem_limit_bytes=56 * 1024 * 1024
+        ),
+    )(
+        state_start.reshape(nc, piece, sw),
+        actions,
+        targets.reshape(targets.shape[0], nc, piece, targets.shape[2]),
+        w_in,
+        w_out,
+        action_embed,
+    )
+
+
 def solution(mesh):
+    nr, nc = mesh.shape["row"], mesh.shape["col"]
+
+    def on_device(state_start, actions, targets, w_in, w_out, action_embed):
+        rb, sw = state_start.shape
+        fits = (
+            targets.shape[0] == 2
+            and nc == 2 * nr
+            and rb % (16 * nc) == 0
+            and sw % 128 == 0
+            and w_in.shape[0] % 128 == 0
+            and w_in.shape[1] % 128 == 0
+        )
+        args = (state_start, actions, targets, w_in, w_out, action_embed)
+        if fits:
+            return stationary(nr, nc, *args)
+        return gathered(*args)
+
     in_specs = (
         P("row", "col"),
         P("row", None),

time: 337 us -> 165 us (0.49)
  waiting for transfers between devices: 214 us -> 0 us
  Pallas kernels: 0 us -> 159 us
  blocking collectives: 57.5 us -> 0 us
  matrix products: 22.8 us -> 0 us
  between operations: 14.3 us -> 0.66 us
  starting transfers between devices: 9.7 us -> 0 us
  other arithmetic: 6.97 us -> 0 us
  local copies, waits for them, and re-layouts: 11 us -> 4.74 us
    pallas_call x0 -> x1, Pallas kernels: none -> 159 us  [stationary(): pl.pallas_call(functools.partial(kernel, nr, nc), out_shape=(jax.ShapeDty...]
    reduce_scatter x3 -> x0, waiting for transfers between devices: 90.3 us -> none  [the longest x2 64.8 us: on_device(): lax.psum_scatter(partial_value.astype(jnp.bfloat16), 'col', scatter_dimen...]
    all_gather x4 -> x0, waiting for transfers between devices: 88.6 us -> none  [the longest x1 44 us: on_device(): w_out_panel = lax.all_gather(w_out, 'row', axis=1, tiled=True)]
    all_gather x4 -> x0, blocking collectives: 45.4 us -> none  [the longest x2 23.6 us: on_device(): full_rows = lax.all_gather(current, 'col', axis=1, tiled=True)]
    all_to_all x2 -> x0, waiting for transfers between devices: 33.4 us -> none  [the longest x1 33.4 us: on_device(): lax.all_to_all(grad_stack, 'row', split_axis=2, concat_axis=1, tiled=True)]
    dot_general x11 -> x0, matrix products: 22.8 us -> none  [the longest x2 5.08 us: on_device(): jnp.dot(hidden, w_out_panel, preferred_element_type=jnp.float32)]
    psum x1 -> x0, blocking collectives: 12.1 us -> none  [shared_cosine(): lax.psum((jnp.sum(state_f * state_f, axis=-1), jnp.sum(state_f * target_f...]
    all_to_all x2 -> x0, starting transfers between devices: 9.5 us -> none  [the longest x1 4.9 us: on_device(): lax.all_to_all(state_stack, 'row', split_axis=2, concat_axis=1, tiled=True)]
  transfers between devices with their start and end apart: 9 -> 0, of which waited for: 7 -> 0; matrix products, arithmetic and copies ran while one was open for 6% -> 0% of each run, Pallas kernels for 0% -> 0%
where the time goes in v1:
time: 165 us; the launch traced here: 164 us
  Pallas kernels  159 us (96%)
  local copies, waits for them, and re-layouts  4.74 us (3%)
    pallas_call x1, Pallas kernels, stationary(): pl.pallas_call(functools.partial(kernel, nr, nc), out_shape=(jax.ShapeDty...  159 us
    unnamed x7, local copies, waits for them, and re-layouts  4.74 us

profile of v1, /device:TPU:0, one launch (start us, length us, event | category | flops | bytes accessed | tf_op | source)
XLA Modules:
  0.0 164.1 jit_solution(15571521208303875204)
XLA Ops:
  0.6 0.0 copy-start.1
  0.6 0.7 copy-done.1
  1.3 0.7 copy.8.act
  2.0 158.7 %shard_map.77 = (f32[512,512]{1,0:T(8,128)}, f32[512,512]{1,0:T(8,128)}) custom-call(bf16[8,16,256]{2,1,0:T(8,128)(2,1)} %bitcast.3, s32[128,2]{1,0:T(8,128)} %copy.8.act, bf16[2,8,16,2048]{3,2,1,0:T(8,128)(2,1)} %bitcast.2, bf16[512,512]{1,0:T(8,128)(2,1)} %wi.1, bf16[512,512]{1,0:T(8,128)(2,1)} %wo.1, bf16[18,512]{1,0:T(8,128)(2,1)} %emb.1), custom_call_target="tpu_custom_call" | custom-call | tf_op jit(solution)/shard_map/pallas_call | solution.py:373
  160.8 0.0 copy-start
  160.8 2.4 %copy.11 = f32[512,512]{1,0:T(8,128)} copy(f32[512,512]{1,0:T(8,128)} %get-tuple-element.4) | data formatting | bytes 2097152
  163.1 0.0 copy-done
  163.1 1.0 copy.12
Async XLA Ops:
  0.6 0.7 copy-start.1
  160.8 2.4 %copy-start = (f32[512,512]{1,0:T(8,128)S(1)}, f32[512,512]{1,0:T(8,128)}, u32[]{:S(2)}) copy-start(f32[512,512]{1,0:T(8,128)} %get-tuple-element.5) | copy-start | bytes 3145732

commit v2 on v0

--- a/solution.py
+++ b/solution.py
@@ -1,10 +1,17 @@
+import functools
+
 import jax
 import jax.numpy as jnp
 from jax import lax
+from jax.experimental import pallas as pl
+from jax.experimental.pallas import tpu as pltpu
 from jax.sharding import PartitionSpec as P
 
 EPS = 1e-06
 LOSS_SCALE = 128.0
+MESH = pl.DeviceIdType.MESH
+F32 = jnp.float32
+BF16 = jnp.bfloat16
 
 
 def silu_grad(pre_act):
@@ -37,7 +44,7 @@
     )
 
 
-def on_device(state_start, actions, targets, w_in, w_out, action_embed):
+def gathered(state_start, actions, targets, w_in, w_out, action_embed):
     unroll_steps = targets.shape[0]
     col_width = state_start.shape[1]
     w_in_panel = lax.all_gather(w_in, "row", axis=0, tiled=True)
@@ -108,7 +115,390 @@
     return (grad_w_in, grad_w_out)
 
 
+def sem_plan(nr, nc):
+    at = {}
+    total = 0
+    for name, count in (
+        [("start", nr), ("targets", nr)]
+        + [(f"cag{i}", nr * nc) for i in range(4)]
+        + [(f"zrs{i}", 2 * nr) for i in range(4)]
+        + [(f"zag{i}", 2 * nr) for i in range(4)]
+        + [(f"crs{i}", nr * nc) for i in range(3)]
+        + [(f"dot{i}", 2 * nr) for i in range(2)]
+    ):
+        at[name] = total
+        total += count
+    return at, total
+
+
+def sends_in_all(nr, nc):
+    per = nc // 2
+    return per + (nr - 1) * (1 + 8 + 8 + 4) + 4 * nr * (nc - 1) + 3 * 2 * nr * per
+
+
+def kernel(
+    nr, nc, st, act, tg, wi, wo, emb, gwi, gwo,
+    s0p, tgp, sfull, hfull, efull, gfull, psend, zr, ysend, cr, own, pre, dsend, dz,
+    send_sem, recv_sem,
+):
+    r, c = lax.axis_index("row"), lax.axis_index("col")
+    piece, df = sfull.shape[3], sfull.shape[4]
+    per, pair = nc // 2, nr // 2
+    rows = per * piece
+    home, half = lax.div(c, 2), lax.rem(c, 2)
+    place, first = lax.div(c, 2), half * pair
+    side = lax.div(r, pair)
+    at, _ = sem_plan(nr, nc)
+    started = []
+    unused = iter(range(10000))
+
+    def zpeer(o):
+        return lax.rem(r + o, nr)
+
+    def cpeer(o):
+        return lax.rem(c + o, nc)
+
+    def copy(src, dst, sem, slot, dev):
+        return pltpu.make_async_remote_copy(
+            src_ref=src, dst_ref=dst, send_sem=send_sem.at[sem], recv_sem=recv_sem.at[slot],
+            device_id=dev, device_id_type=MESH,
+        )
+
+    def send(src, dst, slot, dev, when=None):
+        sem = next(unused)
+        started.append((src, dst, sem, slot, dev, when))
+        if when is None:
+            copy(src, dst, sem, slot, dev).start()
+        else:
+            pl.when(when)(lambda: copy(src, dst, sem, slot, dev).start())
+
+    def arrived(dst, slot, dev, when=None):
+        if when is None:
+            copy(dst, dst, 0, slot, dev).wait_recv()
+        else:
+            pl.when(when)(lambda: copy(dst, dst, 0, slot, dev).wait_recv())
+
+    barrier = pltpu.get_barrier_semaphore()
+    for o in range(1, nr):
+        pl.semaphore_signal(barrier, inc=1, device_id=(zpeer(o), c), device_id_type=MESH)
+    for o in range(1, nc):
+        pl.semaphore_signal(barrier, inc=1, device_id=(r, cpeer(o)), device_id_type=MESH)
+    for hf in range(2):
+        for i in range(pair):
+
+            @pl.when((2 * r + hf != c) | (first + i != r))
+            def _():
+                pl.semaphore_signal(
+                    barrier, inc=1, device_id=(first + i, 2 * r + hf), device_id_type=MESH
+                )
+
+    away = (home != r) | (half != side)
+    pl.semaphore_wait(barrier, (nr - 1) + (nc - 1) + (per - 1) + jnp.where(away, 1, 0))
+
+    mine = half * pair + lax.rem(r, pair)
+    for o in range(per):
+        p = lax.rem(place + o, per)
+        send(
+            st.at[:, p], s0p.at[half, lax.rem(r, pair)], at["start"] + mine,
+            (home, 2 * p + side), away if o == 0 else None,
+        )
+
+    @pl.when(jnp.logical_not(away))
+    def _():
+        s0p[half, lax.rem(r, pair)] = st[:, place]
+
+    for hf in range(2):
+        for i in range(pair):
+            arrived(
+                s0p.at[hf, i], at["start"] + hf * pair + i, (first + i, 2 * r + hf),
+                (2 * r + hf != c) | (first + i != r),
+            )
+
+    order = [zpeer(o) for o in range(1, nr)] + [r]
+    back_order = [r] + [zpeer(o) for o in range(1, nr)]
+
+    def spread(full, name, i, k):
+        b, q = first + i, per * k + place
+        for o in range(1, nc):
+            send(full.at[b, q], full.at[b, q], at[name] + b * nc + q, (r, cpeer(o)))
+
+    def collect(full, name, b, k):
+        for o in range(per):
+            p = lax.rem(place + o, per)
+            q = per * k + p
+            arrived(
+                full.at[b, q], at[name] + b * nc + q, (r, 2 * p + lax.div(b, pair)),
+                lax.div(b, pair) != half if o == 0 else None,
+            )
+
+    def mm(a, b, dims):
+        return lax.dot_general(a, b, (dims, ((), ())), preferred_element_type=F32)
+
+    def block(full, b, k):
+        return full[b, per * k:per * (k + 1)].reshape(rows, df)
+
+    def reduce_rows(full, name, weight, dims, phase, k):
+        for o in range(1, nr):
+            b = zpeer(o)
+            collect(full, name, b, k)
+            psend[phase, b, k] = mm(block(full, b, k), weight[...], dims).astype(BF16)
+            send(
+                psend.at[phase, b, k], zr.at[phase, r, k],
+                at[f"zrs{phase}"] + 2 * r + k, (b, c),
+            )
+        collect(full, name, r, k)
+        return mm(block(full, r, k), weight[...], dims)
+
+    def reduced(total, phase, k):
+        for o in range(nr - 1, 0, -1):
+            b = zpeer(o)
+            arrived(zr.at[phase, b, k], at[f"zrs{phase}"] + 2 * b + k, (b, c))
+            total = total + zr[phase, b, k].astype(F32)
+        return total
+
+    def share_rows(full, phase, k):
+        for o in range(1, nr):
+            send(full.at[r, k], full.at[r, k], at[f"zag{phase}"] + 2 * r + k, (zpeer(o), c))
+
+    def shared(full, phase, b, k):
+        arrived(full.at[b, k], at[f"zag{phase}"] + 2 * b + k, (b, c))
+
+    def group_terms(full, zphase, weight, dims, phase, k):
+        for b in [r] + [zpeer(o) for o in range(nr - 1, 0, -1)]:
+            if b is not r:
+                shared(full, zphase, b, k)
+            term = mm(full[b, k], weight[...], dims).astype(BF16)
+            ysend[phase, b, per * k:per * (k + 1)] = term.reshape(per, piece, df)
+            slot = at[f"crs{phase}"] + (lax.rem(b, pair) * 2 + k) * nc + c
+            for o in range(per - 1, -1, -1):
+                p = lax.rem(place + o, per)
+                send(
+                    ysend.at[phase, b, per * k + p], cr.at[phase, lax.rem(b, pair), k, c], slot,
+                    (r, 2 * p + lax.div(b, pair)),
+                    lax.div(b, pair) != half if o == 0 else None,
+                )
+
+    def group_total(phase, i, k):
+        total = ysend[phase, first + i, per * k + place].astype(F32)
+        for o in range(1, nc):
+            j = cpeer(o)
+            arrived(cr.at[phase, i, k, j], at[f"crs{phase}"] + (i * 2 + k) * nc + j, (r, j))
+            total = total + cr[phase, i, k, j].astype(F32)
+        return total
+
+    lane = lax.broadcasted_iota(jnp.int32, (piece, 128), 1)
+
+    def dots(u, k):
+        for i in range(pair):
+            s = own[u, i, k].astype(F32)
+            t = tgp[i, u, k].astype(F32)
+            ss = jnp.sum(s * s, axis=-1, keepdims=True)
+            sc = jnp.sum(s * t, axis=-1, keepdims=True)
+            tt = jnp.sum(t * t, axis=-1, keepdims=True)
+            both = jnp.where(lane == 0, ss, jnp.where(lane == 1, sc, tt))
+            dsend[u, k, i] = both
+            dz[u, k, r, i] = both
+        for o in range(1, nr):
+            send(dsend.at[u, k], dz.at[u, k, r], at[f"dot{u}"] + 2 * r + k, (zpeer(o), c))
+
+    def dots_in(u, k):
+        for o in range(1, nr):
+            b = zpeer(o)
+            arrived(dz.at[u, k, b], at[f"dot{u}"] + 2 * b + k, (b, c))
+
+    def cosine(u, i, k):
+        total = dz[u, k, 0, i]
+        for z in range(1, nr):
+            total = total + dz[u, k, z, i]
+        return cosine_from(
+            own[u, i, k].astype(F32), tgp[i, u, k].astype(F32),
+            total[:, 0:1], total[:, 1:2], total[:, 2:3],
+        )
+
+    ids = lax.broadcasted_iota(jnp.int32, (rows, emb.shape[0]), 1)
+    plain, flipped, over_rows = ((1,), (0,)), ((1,), (1,)), ((0,), (0,))
+
+    def into_hidden(u, k):
+        total = reduce_rows(sfull.at[u], f"cag{u}", wi, plain, u, k)
+        onehot = (act[rows * k:rows * (k + 1), u:u + 1] == ids).astype(F32).astype(BF16)
+        pre[u, k] = total + mm(onehot, emb[...], plain)
+
+    def hidden(u, k):
+        total = reduced(pre[u, k], u, k)
+        pre[u, k] = total
+        hfull[u, r, k] = (total * jax.nn.sigmoid(total)).astype(BF16)
+        share_rows(hfull.at[u], u, k)
+
+    def next_state(u, k):
+        for i in range(pair):
+            old = sfull[u, first + i, per * k + place].astype(F32)
+            new = (old + group_total(u, i, k)).astype(BF16)
+            own[u, i, k] = new
+            if u == 0:
+                sfull[1, first + i, per * k + place] = new
+                spread(sfull.at[1], "cag1", i, k)
+
+    def last_grad(k):
+        dots_in(1, k)
+        for i in range(pair):
+            gfull[1, first + i, per * k + place] = cosine(1, i, k).astype(BF16)
+            spread(gfull.at[1], "cag2", i, k)
+
+    def into_back(u, k):
+        back[k] = reduce_rows(gfull.at[u], f"cag{3 - u}", wo, flipped, 3 - u, k)
+
+    def hidden_grad(u, k):
+        total = reduced(back[k], 3 - u, k)
+        efull[u, r, k] = (total * silu_grad(pre[u, k])).astype(BF16)
+        share_rows(efull.at[u], 3 - u, k)
+
+    def first_grad(k):
+        dots_in(0, k)
+        for i in range(pair):
+            b, q = first + i, per * k + place
+            summed = gfull[1, b, q].astype(F32) + group_total(2, i, k) + cosine(0, i, k)
+            gfull[0, b, q] = summed.astype(BF16)
+            spread(gfull.at[0], "cag3", i, k)
+
+    back = [None, None]
+    for k in range(2):
+        for i in range(pair):
+            sfull[0, first + i, per * k + place] = jnp.concatenate(
+                [s0p[0, i, k], s0p[1, i, k]], axis=-1
+            )
+            spread(sfull.at[0], "cag0", i, k)
+    into_hidden(0, 0)
+    into_hidden(0, 1)
+
+    for o in range(1, nr):
+        b = zpeer(o)
+        send(
+            tg.at[:, :, place, :, pl.ds(pl.multiple_of(b * df, df), df)],
+            tgp.at[lax.rem(r, pair)], at["targets"] + lax.rem(r, pair), (b, c), side == half,
+        )
+
+    @pl.when(side == half)
+    def _():
+        tgp[lax.rem(r, pair)] = tg[:, :, place, :, pl.ds(pl.multiple_of(r * df, df), df)]
+
+    hidden(0, 0)
+    hidden(0, 1)
+    group_terms(hfull.at[0], 0, wo, plain, 0, 0)
+    next_state(0, 0)
+    group_terms(hfull.at[0], 0, wo, plain, 0, 1)
+    into_hidden(1, 0)
+    next_state(0, 1)
+    into_hidden(1, 1)
+    for i in range(pair):
+        arrived(tgp.at[i], at["targets"] + i, (first + i, c), first + i != r)
+    hidden(1, 0)
+    hidden(1, 1)
+    dots(0, 0)
+    dots(0, 1)
+    group_terms(hfull.at[1], 1, wo, plain, 1, 0)
+    next_state(1, 0)
+    dots(1, 0)
+    group_terms(hfull.at[1], 1, wo, plain, 1, 1)
+    last_grad(0)
+    next_state(1, 1)
+    dots(1, 1)
+    into_back(1, 0)
+    last_grad(1)
+    into_back(1, 1)
+    hidden_grad(1, 0)
+    hidden_grad(1, 1)
+    group_terms(efull.at[1], 2, wi, flipped, 2, 0)
+    first_grad(0)
+    group_terms(efull.at[1], 2, wi, flipped, 2, 1)
+    into_back(0, 0)
+    first_grad(1)
+    into_back(0, 1)
+
+    def tall(x):
+        return x.reshape(nr * nc * piece, x.shape[-1])
+
+    hidden_grad(0, 0)
+    hidden_grad(0, 1)
+    gwo[...] = mm(tall(hfull[1]), tall(gfull[1]), over_rows)
+    gwi[...] = mm(tall(sfull[1]), tall(efull[1]), over_rows)
+    gwo[...] += mm(tall(hfull[0]), tall(gfull[0]), over_rows)
+    for k in range(2):
+        for b in order[:-1]:
+            shared(efull.at[0], 3, b, k)
+    gwi[...] += mm(tall(sfull[0]), tall(efull[0]), over_rows)
+
+    for src, dst, sem, slot, dev, when in started:
+        if when is None:
+            copy(src, dst, sem, slot, dev).wait_send()
+        else:
+            pl.when(when)(lambda: copy(src, dst, sem, slot, dev).wait_send())
+
+
+def stationary(nr, nc, state_start, actions, targets, w_in, w_out, action_embed):
+    rb, sw = state_start.shape
+    piece = rb // nc
+    per, pair, rows = nc // 2, nr // 2, rb // 2
+    df, fc = w_in.shape
+    vm = pl.BlockSpec(memory_space=pltpu.VMEM)
+    _, receives = sem_plan(nr, nc)
+    return pl.pallas_call(
+        functools.partial(kernel, nr, nc),
+        out_shape=(
+            jax.ShapeDtypeStruct((df, fc), F32),
+            jax.ShapeDtypeStruct((fc, df), F32),
+        ),
+        in_specs=[vm] * 6,
+        out_specs=(vm, vm),
+        scratch_shapes=[
+            pltpu.VMEM((2, pair, 2, piece, sw), BF16),
+            pltpu.VMEM((pair, 2, 2, piece, df), BF16),
+            pltpu.VMEM((2, nr, nc, piece, df), BF16),
+            pltpu.VMEM((2, nr, 2, rows, fc), BF16),
+            pltpu.VMEM((2, nr, 2, rows, fc), BF16),
+            pltpu.VMEM((2, nr, nc, piece, df), BF16),
+            pltpu.VMEM((4, nr, 2, rows, fc), BF16),
+            pltpu.VMEM((4, nr, 2, rows, fc), BF16),
+            pltpu.VMEM((3, nr, nc, piece, df), BF16),
+            pltpu.VMEM((3, pair, 2, nc, piece, df), BF16),
+            pltpu.VMEM((2, pair, 2, piece, df), BF16),
+            pltpu.VMEM((2, 2, rows, fc), F32),
+            pltpu.VMEM((2, 2, pair, piece, 128), F32),
+            pltpu.VMEM((2, 2, nr, pair, piece, 128), F32),
+            pltpu.SemaphoreType.DMA((sends_in_all(nr, nc),)),
+            pltpu.SemaphoreType.DMA((receives,)),
+        ],
+        compiler_params=pltpu.CompilerParams(
+            collective_id=0, has_side_effects=True, vmem_limit_bytes=56 * 1024 * 1024
+        ),
+    )(
+        state_start.reshape(2, per, piece, sw),
+        actions,
+        targets.reshape(targets.shape[0], 2, per, piece, targets.shape[2]),
+        w_in,
+        w_out,
+        action_embed,
+    )
+
+
 def solution(mesh):
+    nr, nc = mesh.shape["row"], mesh.shape["col"]
+
+    def on_device(state_start, actions, targets, w_in, w_out, action_embed):
+        rb, sw = state_start.shape
+        fits = (
+            targets.shape[0] == 2
+            and nc == 2 * nr
+            and nr % 2 == 0
+            and rb % (16 * nc) == 0
+            and sw % 128 == 0
+            and w_in.shape[0] % 128 == 0
+            and w_in.shape[1] % 128 == 0
+        )
+        args = (state_start, actions, targets, w_in, w_out, action_embed)
+        if fits:
+            return stationary(nr, nc, *args)
+        return gathered(*args)
+
     in_specs = (
         P("row", "col"),
         P("row", None),

time: 337 us -> 146 us (0.43)
  waiting for transfers between devices: 214 us -> 0 us
  Pallas kernels: 0 us -> 139 us
  blocking collectives: 57.5 us -> 0 us
  matrix products: 22.8 us -> 0 us
  between operations: 14.3 us -> 0.66 us
  starting transfers between devices: 9.7 us -> 0 us
  other arithmetic: 6.97 us -> 0 us
  local copies, waits for them, and re-layouts: 11 us -> 4.74 us
    pallas_call x0 -> x1, Pallas kernels: none -> 139 us  [stationary(): pl.pallas_call(functools.partial(kernel, nr, nc), out_shape=(jax.ShapeDty...]
    reduce_scatter x3 -> x0, waiting for transfers between devices: 90.3 us -> none  [the longest x2 64.8 us: on_device(): lax.psum_scatter(partial_value.astype(jnp.bfloat16), 'col', scatter_dimen...]
    all_gather x4 -> x0, waiting for transfers between devices: 88.6 us -> none  [the longest x1 44 us: on_device(): w_out_panel = lax.all_gather(w_out, 'row', axis=1, tiled=True)]
    all_gather x4 -> x0, blocking collectives: 45.4 us -> none  [the longest x2 23.6 us: on_device(): full_rows = lax.all_gather(current, 'col', axis=1, tiled=True)]
    all_to_all x2 -> x0, waiting for transfers between devices: 33.4 us -> none  [the longest x1 33.4 us: on_device(): lax.all_to_all(grad_stack, 'row', split_axis=2, concat_axis=1, tiled=True)]
    dot_general x11 -> x0, matrix products: 22.8 us -> none  [the longest x2 5.08 us: on_device(): jnp.dot(hidden, w_out_panel, preferred_element_type=jnp.float32)]
    psum x1 -> x0, blocking collectives: 12.1 us -> none  [shared_cosine(): lax.psum((jnp.sum(state_f * state_f, axis=-1), jnp.sum(state_f * target_f...]
    all_to_all x2 -> x0, starting transfers between devices: 9.5 us -> none  [the longest x1 4.9 us: on_device(): lax.all_to_all(state_stack, 'row', split_axis=2, concat_axis=1, tiled=True)]
  transfers between devices with their start and end apart: 9 -> 0, of which waited for: 7 -> 0; matrix products, arithmetic and copies ran while one was open for 6% -> 0% of each run, Pallas kernels for 0% -> 0%
where the time goes in v2:
time: 146 us; the launch traced here: 145 us
  Pallas kernels  139 us (95%)
  local copies, waits for them, and re-layouts  4.74 us (3%)
    pallas_call x1, Pallas kernels, stationary(): pl.pallas_call(functools.partial(kernel, nr, nc), out_shape=(jax.ShapeDty...  139 us
    unnamed x7, local copies, waits for them, and re-layouts  4.74 us

profile of v2, /device:TPU:0, one launch (start us, length us, event | category | flops | bytes accessed | tf_op | source)
XLA Modules:
  0.0 144.8 jit_solution(16708161500940400801)
XLA Ops:
  0.6 0.0 copy-start.1
  0.6 0.7 copy-done.1
  1.3 0.7 copy.8.act
  2.0 139.4 %shard_map.77 = (f32[512,512]{1,0:T(8,128)}, f32[512,512]{1,0:T(8,128)}) custom-call(bf16[2,4,16,256]{3,2,1,0:T(8,128)(2,1)} %bitcast.3, s32[128,2]{1,0:T(8,128)} %copy.8.act, bf16[2,2,4,16,2048]{4,3,2,1,0:T(8,128)(2,1)} %bitcast.2, bf16[512,512]{1,0:T(8,128)(2,1)} %wi.1, bf16[512,512]{1,0:T(8,128)(2,1)} %wo.1, bf16[18,512]{1,0:T(8,128)(2,1)} %emb.1), custom_call_target="tpu_custom_call" | custom-call | tf_op jit(solution)/shard_map/pallas_call | solution.py:444
  141.5 0.0 copy-start
  141.5 2.4 %copy.11 = f32[512,512]{1,0:T(8,128)} copy(f32[512,512]{1,0:T(8,128)} %get-tuple-element.4) | data formatting | bytes 2097152
  143.8 0.0 copy-done
  143.8 1.0 copy.12
Async XLA Ops:
  0.6 0.7 copy-start.1
  141.5 2.4 %copy-start = (f32[512,512]{1,0:T(8,128)S(1)}, f32[512,512]{1,0:T(8,128)}, u32[]{:S(2)}) copy-start(f32[512,512]{1,0:T(8,128)} %get-tuple-element.5) | copy-start | bytes 3145732
